TPU v7x, 32 devices: a whole 2x2x4 slice. The times are simulated.
32 devices in a mesh: dp: 8 (over z, x), ctx: 4 (over y, core).
Axes of the slice: x: 2, y: 2, z: 4, core: 2. Of those that a mesh axis runs over, the one named last changes fastest.
Arguments:
- tokens: bfloat16 [16, 1024, 768], P('dp', 'ctx'), may hold values from -6 to 6
- segment_ids: int32 [16, 1024], P('dp', 'ctx'), may hold values from 0 to 3, never falling along the last dimension, each value on 1 to 512 neighbouring positions
- cotangent: bfloat16 [16, 1024, 768], P('dp', 'ctx'), may hold values from -6 to 6
- w_in: float32 [768, 3352], P(('dp', 'ctx')), may hold values from -0.21875 to 0.21875
- w_out: float32 [1536, 768], P(('dp', 'ctx')), may hold values from -0.15625 to 0.15625
- mom_in: float32 [768, 3352], P(('dp', 'ctx')), may hold values from -128 to 128
- mom_out: float32 [1536, 768], P(('dp', 'ctx')), may hold values from -640 to 640
- pre_gain: float32 [768], replicated, may hold values from 0.5 to 1.5
- conv_weight: float32 [4, 1792], replicated, may hold values from -3 to 3
- conv_bias: float32 [1792], replicated, may hold values from -6 to 6
- dt_bias: float32 [24], replicated, may hold values from -5 to -3
- a_log: float32 [24], replicated, may hold values from -3.5 to 1.1
- d_skip: float32 [24], replicated, may hold values from 0.5 to 1.5
- norm_gain: float32 [1536], replicated, may hold values from 0.5 to 1.5
Outputs:
- mixed: bfloat16 [16, 1024, 768], P('dp', 'ctx')
- d_tokens: bfloat16 [16, 1024, 768], P('dp', 'ctx')
- grad_w_in: float32 [768, 3352], P(('dp', 'ctx'))
- grad_w_out: float32 [1536, 768], P(('dp', 'ctx'))
- grad_pre_gain: float32 [768], replicated
- grad_conv_weight: float32 [4, 1792], replicated
- grad_conv_bias: float32 [1792], replicated
- grad_dt_bias: float32 [24], replicated
- grad_a_log: float32 [24], replicated
- grad_d_skip: float32 [24], replicated
- grad_norm_gain: float32 [1536], replicated
- new_w_in: float32 [768, 3352], P(('dp', 'ctx'))
- new_w_out: float32 [1536, 768], P(('dp', 'ctx'))
- new_mom_in: float32 [768, 3352], P(('dp', 'ctx'))
- new_mom_out: float32 [1536, 768], P(('dp', 'ctx'))
- new_pre_gain: float32 [768], replicated
- new_conv_weight: float32 [4, 1792], replicated
- new_conv_bias: float32 [1792], replicated
- new_dt_bias: float32 [24], replicated
- new_a_log: float32 [24], replicated
- new_d_skip: float32 [24], replicated
- new_norm_gain: float32 [1536], replicated
Inputs may be any that keep to these rules, and one draw needn't show every extreme that they name: `segment_ids`: segment numbers never fall along a sequence; each document has 1 to 512 tokens and one has exactly 512.
All inputs are finite; a program needn't handle non-finite values.
Results may differ from a plain program's by a relative error of at most 0.01.
Values may be sent and summed in bfloat16 or wider, within the bound.
No kernel may reach another device: no remote copies, remote signals or barrier semaphores. Data moves between devices by JAX's collectives and lax.ppermute only.
A program may use at most 192 MiB of HBM per device.

v0:
```python
from functools import partial
import math
import jax
import jax.numpy as jnp
from jax import lax
from jax.sharding import PartitionSpec as P

D = 768
HEADS = 24
HEADDIM = 64
NSTATE = 128
CONVK = 4
MICRO = 2
SEQ_MB = 1
DI = 1536
CONVD = 1792
EPROJ = 3352
norm_eps = 1e-05
coef_a = 3.4445
coef_b = -4.775
coef_c = 2.0315
momentum_rate = 0.95
muon_rate = 0.05
plain_rate = 0.003


def from_behind(block, axis, distance):
    devices = range(lax.axis_size(axis))
    route = [(i - distance, i) for i in devices if i - distance in devices]
    return lax.ppermute(block, axis, route)


def prefix(shard, axis, combine, identity):
    peers, here = (lax.axis_size(axis), lax.axis_index(axis))
    everything = jax.tree.map(
        lambda part, kind: lax.all_gather(part.astype(kind), axis),
        shard,
        (jnp.bfloat16, jnp.bfloat16),
    )
    start = jax.tree.map(
        lambda part, zero: jnp.broadcast_to(jnp.asarray(zero, part.dtype), part.shape),
        shard,
        identity,
    )

    def step(k, before):
        reached = k < here
        new = combine(
            before, jax.tree.map(lambda part, own: part[k].astype(own.dtype), everything, shard)
        )
        return jax.tree.map(lambda a, b: jnp.where(reached, a, b), new, before)

    return lax.fori_loop(0, peers, step, start)


def prefix_2(shard, axis, combine, identity):
    peers, here = (lax.axis_size(axis), lax.axis_index(axis))
    everything = jax.tree.map(
        lambda part, kind: lax.all_gather(part.astype(kind), axis),
        shard,
        jax.tree.map(lambda a: jnp.bfloat16 if a.dtype == jnp.float32 else a.dtype, shard),
    )
    start = jax.tree.map(
        lambda part, zero: jnp.broadcast_to(jnp.asarray(zero, part.dtype), part.shape),
        shard,
        identity,
    )

    def step(k, before):
        at = peers - 1 - k
        reached = at > here
        new = combine(
            before, jax.tree.map(lambda part, own: part[at].astype(own.dtype), everything, shard)
        )
        return jax.tree.map(lambda a, b: jnp.where(reached, a, b), new, before)

    return lax.fori_loop(0, peers, step, start)


def pre_norm(x_float, gain_vec):
    mean_sq = jnp.mean(x_float * x_float, axis=-1, keepdims=True)
    return x_float * lax.rsqrt(mean_sq + norm_eps) * gain_vec


def make_masks(seg_float, rim_seg):
    block_len = seg_float.shape[1]
    causal = jnp.arange(block_len)[:, None] >= jnp.arange(block_len)[None, :]
    same_seg = jnp.where(
        causal[None], seg_float[:, :, None] == seg_float[:, None, :], False
    ).astype(jnp.float32)
    end_same = (seg_float == seg_float[:, -1:]).astype(jnp.float32)
    carry_mask = (seg_float == rim_seg[:, -1:]).astype(jnp.float32)
    seg_ext = jnp.concatenate([rim_seg, seg_float], axis=1)
    tap_masks = tuple(
        (
            (seg_ext[:, tap_idx : tap_idx + block_len] == seg_float).astype(jnp.float32)
            for tap_idx in range(CONVK - 1)
        )
    )
    return (same_seg, end_same, carry_mask, tap_masks)


def block_mid(seg_masks, conv_in, dt_raw, rim_vals, conv_weight, conv_bias, dt_bias, a_log):
    same_seg, end_same, carry_mask, tap_masks = seg_masks
    batch_rows = conv_in.shape[0]
    block_len = conv_in.shape[1]
    extended = jnp.concatenate([rim_vals, conv_in], axis=1)
    conv_sum = conv_bias + conv_weight[CONVK - 1] * conv_in
    for tap_idx in range(CONVK - 1):
        conv_sum = (
            conv_sum
            + conv_weight[tap_idx]
            * extended[:, tap_idx : tap_idx + block_len, :]
            * tap_masks[tap_idx][..., None]
        )
    activated = jax.nn.silu(conv_sum)
    x_heads = activated[..., :DI].reshape(batch_rows, block_len, HEADS, HEADDIM)
    b_state = activated[..., DI : DI + NSTATE]
    c_state = activated[..., DI + NSTATE :]
    dt_step = jax.nn.softplus(dt_raw + dt_bias)
    log_decay = -dt_step * jnp.exp(a_log)
    cum_decay = jnp.cumsum(log_decay, axis=1)
    block_decay = jnp.exp(cum_decay[:, -1, :]) * carry_mask[:, -1:]
    end_weights = jnp.exp(cum_decay[:, -1:, :] - cum_decay) * end_same[..., None] * dt_step
    local_state = jnp.einsum(
        "bqh,bqhp,bqn->bhpn", end_weights, x_heads, b_state, precision=lax.Precision.HIGHEST
    )
    return (block_decay, local_state, x_heads, b_state, c_state, dt_step, cum_decay)


def block_out(
    seg_masks, x_heads, b_state, c_state, dt_step, cum_decay, incoming, gate_in, d_skip, norm_gain
):
    same_seg, end_same, carry_mask, tap_masks = seg_masks
    batch_rows = x_heads.shape[0]
    block_len = x_heads.shape[1]
    scores = jnp.einsum("btn,bsn->bts", c_state, b_state, precision=lax.Precision.HIGHEST)
    cum_heads = jnp.swapaxes(cum_decay, 1, 2)
    decay_gap = cum_heads[:, :, :, None] - cum_heads[:, :, None, :]
    keep_mask = same_seg[:, None]
    decay_mat = jnp.exp(jnp.where(keep_mask > 0, decay_gap, 0.0)) * keep_mask
    weight = decay_mat * scores[:, None] * jnp.swapaxes(dt_step, 1, 2)[:, :, None, :]
    y_inner = jnp.einsum("bhts,bshp->bthp", weight, x_heads, precision=lax.Precision.HIGHEST)
    y_carry = jnp.einsum("btn,bhpn->bthp", c_state, incoming, precision=lax.Precision.HIGHEST)
    y_carry = y_carry * (jnp.exp(cum_decay) * carry_mask[..., None])[..., None]
    y_heads = y_inner + y_carry + d_skip[:, None] * x_heads
    gated = y_heads.reshape(batch_rows, block_len, DI) * jax.nn.silu(gate_in)
    return gated * lax.rsqrt(jnp.mean(gated * gated, axis=-1, keepdims=True) + norm_eps) * norm_gain


def combine_states(before_part, after_part):
    return (
        before_part[0] * after_part[0],
        after_part[0][..., None, None] * before_part[1] + after_part[1],
    )


def orthogonal(matrix_low):
    frobenius = jnp.sqrt(jnp.sum(jnp.square(matrix_low.astype(jnp.float32))))
    current = (matrix_low.astype(jnp.float32) / (frobenius + 1e-07)).astype(jnp.bfloat16)
    for turn_idx in range(5):
        gram_mat = jnp.dot(current, current.T, preferred_element_type=jnp.float32).astype(
            jnp.bfloat16
        )
        poly_mat = coef_b * gram_mat.astype(jnp.float32) + coef_c * jnp.dot(
            gram_mat, gram_mat, preferred_element_type=jnp.float32
        )
        poly_mat = poly_mat.astype(jnp.bfloat16)
        current = (
            coef_a * current.astype(jnp.float32)
            + jnp.dot(poly_mat, current, preferred_element_type=jnp.float32)
        ).astype(jnp.bfloat16)
    return current


def body(
    tokens,
    segment_ids,
    cotangent,
    w_in,
    w_out,
    mom_in,
    mom_out,
    pre_gain,
    conv_weight,
    conv_bias,
    dt_bias,
    a_log,
    d_skip,
    norm_gain,
):
    win_low = w_in.astype(jnp.bfloat16)
    wout_low = w_out.astype(jnp.bfloat16)
    block_len = tokens.shape[1]
    rim_rows = CONVK - 1
    stored = []
    mixed_parts = []
    for micro_idx in range(MICRO):
        micro_rows = slice(micro_idx * SEQ_MB, (micro_idx + 1) * SEQ_MB)
        full_in, full_out = (
            lax.all_gather(win_low, ("dp", "ctx"), axis=0, tiled=True),
            lax.all_gather(wout_low, ("dp", "ctx"), axis=0, tiled=True),
        )
        x_float = tokens[micro_rows].astype(jnp.float32)
        seg_float = segment_ids[micro_rows].astype(jnp.float32)
        normed, back_pre = jax.vjp(pre_norm, x_float, pre_gain)
        normed_low = normed.astype(jnp.bfloat16).reshape(-1, D)
        projected = jnp.dot(normed_low, full_in, preferred_element_type=jnp.float32).astype(
            jnp.bfloat16
        )
        projected = projected.reshape(SEQ_MB, block_len, EPROJ)
        gate_in = projected[..., :DI].astype(jnp.float32)
        conv_in = projected[..., DI : DI + CONVD].astype(jnp.float32)
        dt_raw = projected[..., DI + CONVD :].astype(jnp.float32)
        rim_vals, rim_seg = from_behind(
            (conv_in[:, block_len - rim_rows :, :], seg_float[:, block_len - rim_rows :]), "ctx", 1
        )
        seg_masks = make_masks(seg_float, rim_seg)
        mid_out, back_mid = jax.vjp(
            partial(block_mid, seg_masks),
            conv_in,
            dt_raw,
            rim_vals,
            conv_weight,
            conv_bias,
            dt_bias,
            a_log,
        )
        block_decay = mid_out[0]
        local_state = mid_out[1]
        identity = (jnp.ones_like(block_decay), jnp.zeros_like(local_state))
        incoming = prefix((block_decay, local_state), "ctx", combine_states, identity)[1]
        gated_normed, back_out = jax.vjp(
            partial(block_out, seg_masks),
            mid_out[2],
            mid_out[3],
            mid_out[4],
            mid_out[5],
            mid_out[6],
            incoming,
            gate_in,
            d_skip,
            norm_gain,
        )
        gated_low = gated_normed.astype(jnp.bfloat16).reshape(-1, DI)
        result = (
            jnp.dot(gated_low, full_out, preferred_element_type=jnp.float32).reshape(
                SEQ_MB, block_len, D
            )
            + x_float
        )
        mixed_parts.append(result.astype(jnp.bfloat16))
        stored.append((normed_low, gated_low, back_pre, back_mid, back_out, block_decay, incoming))
    acc_in = jnp.zeros((D, EPROJ), jnp.float32)
    acc_out = jnp.zeros((DI, D), jnp.float32)
    acc_pre = jnp.zeros_like(pre_gain)
    acc_convw = jnp.zeros_like(conv_weight)
    acc_convb = jnp.zeros_like(conv_bias)
    acc_dtb = jnp.zeros_like(dt_bias)
    acc_alog = jnp.zeros_like(a_log)
    acc_skip = jnp.zeros_like(d_skip)
    acc_norm = jnp.zeros_like(norm_gain)
    grad_parts = [None] * MICRO
    for micro_idx in reversed(range(MICRO)):
        micro_rows = slice(micro_idx * SEQ_MB, (micro_idx + 1) * SEQ_MB)
        full_in, full_out = (
            lax.all_gather(win_low, ("dp", "ctx"), axis=0, tiled=True),
            lax.all_gather(wout_low, ("dp", "ctx"), axis=0, tiled=True),
        )
        normed_low, gated_low, back_pre, back_mid, back_out, block_decay, incoming = stored[
            micro_idx
        ]
        cot_low = cotangent[micro_rows]
        cot_flat = cot_low.reshape(-1, D)
        acc_out = acc_out + jnp.einsum(
            "td,te->de", gated_low, cot_flat, preferred_element_type=jnp.float32
        )
        grad_gated = jnp.einsum(
            "te,de->td", cot_flat, full_out, preferred_element_type=jnp.float32
        ).reshape(SEQ_MB, block_len, DI)
        g_xh, g_bstate, g_cstate, g_dt, g_cum, g_incoming, g_gate, g_skip, g_norm = back_out(
            grad_gated
        )
        identity = (jnp.ones_like(block_decay), jnp.zeros_like(g_incoming))
        carried = prefix_2((block_decay, g_incoming), "ctx", combine_states, identity)[1]
        g_decay = jnp.sum(carried * incoming, axis=(2, 3))
        g_conv, g_dtraw, g_rim, g_convw, g_convb, g_dtb, g_alog = back_mid(
            (g_decay, carried, g_xh, g_bstate, g_cstate, g_dt, g_cum)
        )
        from_next = from_behind(g_rim, "ctx", -1)
        g_conv = jnp.concatenate(
            [g_conv[:, : block_len - rim_rows], g_conv[:, block_len - rim_rows :] + from_next],
            axis=1,
        )
        g_proj = (
            jnp.concatenate([g_gate, g_conv, g_dtraw], axis=-1)
            .astype(jnp.bfloat16)
            .reshape(-1, EPROJ)
        )
        acc_in = acc_in + jnp.einsum(
            "td,te->de", normed_low, g_proj, preferred_element_type=jnp.float32
        )
        g_normed = jnp.einsum(
            "te,de->td", g_proj, full_in, preferred_element_type=jnp.float32
        ).reshape(SEQ_MB, block_len, D)
        g_x, g_pre = back_pre(g_normed)
        grad_parts[micro_idx] = (cot_low.astype(jnp.float32) + g_x).astype(jnp.bfloat16)
        acc_pre = acc_pre + g_pre
        acc_convw = acc_convw + g_convw
        acc_convb = acc_convb + g_convb
        acc_dtb = acc_dtb + g_dtb
        acc_alog = acc_alog + g_alog
        acc_skip = acc_skip + g_skip
        acc_norm = acc_norm + g_norm
    sum_in, sum_out = (
        lax.psum_scatter(acc_in, ("dp", "ctx"), scatter_dimension=0, tiled=True),
        lax.psum_scatter(acc_out, ("dp", "ctx"), scatter_dimension=0, tiled=True),
    )
    smalls = lax.psum(
        (acc_pre, acc_convw, acc_convb, acc_dtb, acc_alog, acc_skip, acc_norm), ("dp", "ctx")
    )
    next_mom_in = momentum_rate * mom_in + sum_in
    next_mom_out = momentum_rate * mom_out + sum_out
    gathered_in, gathered_out = (
        lax.all_gather(next_mom_in.astype(jnp.bfloat16), ("dp", "ctx"), axis=0, tiled=True),
        lax.all_gather(next_mom_out.astype(jnp.bfloat16), ("dp", "ctx"), axis=0, tiled=True),
    )
    position = lax.axis_index(("dp", "ctx"))
    rows_in = w_in.shape[0]
    rows_out = w_out.shape[0]
    ortho_in = orthogonal(gathered_in)
    ortho_out_full = orthogonal(gathered_out.T).T
    mine_in = lax.dynamic_slice_in_dim(ortho_in, position * rows_in, rows_in, 0)
    mine_out = lax.dynamic_slice_in_dim(ortho_out_full, position * rows_out, rows_out, 0)
    new_w_in = w_in - muon_rate * 0.2 * math.sqrt(max(D, EPROJ)) * mine_in.astype(jnp.float32)
    new_w_out = w_out - muon_rate * 0.2 * math.sqrt(max(DI, D)) * mine_out.astype(jnp.float32)
    grad_pre, grad_convw, grad_convb, grad_dtb, grad_alog, grad_skip, grad_norm = smalls
    return (
        jnp.concatenate(mixed_parts, axis=0),
        jnp.concatenate(grad_parts, axis=0),
        sum_in,
        sum_out,
        grad_pre,
        grad_convw,
        grad_convb,
        grad_dtb,
        grad_alog,
        grad_skip,
        grad_norm,
        new_w_in,
        new_w_out,
        next_mom_in,
        next_mom_out,
        pre_gain - plain_rate * grad_pre,
        conv_weight - plain_rate * grad_convw,
        conv_bias - plain_rate * grad_convb,
        dt_bias - plain_rate * grad_dtb,
        a_log - plain_rate * grad_alog,
        d_skip - plain_rate * grad_skip,
        norm_gain - plain_rate * grad_norm,
    )


def solution(mesh):
    return jax.shard_map(
        body,
        mesh=mesh,
        in_specs=(
            P("dp", "ctx", None),
            P("dp", "ctx"),
            P("dp", "ctx", None),
            P(("dp", "ctx"), None),
            P(("dp", "ctx"), None),
            P(("dp", "ctx"), None),
            P(("dp", "ctx"), None),
            P(),
            P(),
            P(),
            P(),
            P(),
            P(),
            P(),
        ),
        out_specs=(
            P("dp", "ctx", None),
            P("dp", "ctx", None),
            P(("dp", "ctx"), None),
            P(("dp", "ctx"), None),
            P(),
            P(),
            P(),
            P(),
            P(),
            P(),
            P(),
            P(("dp", "ctx"), None),
            P(("dp", "ctx"), None),
            P(("dp", "ctx"), None),
            P(("dp", "ctx"), None),
            P(),
            P(),
            P(),
            P(),
            P(),
            P(),
            P(),
        ),
        check_vma=False,
    )
```

profile of v0, /device:TPU:0, one launch (start us, length us, event | category | flops | bytes accessed | tf_op | source)
XLA Modules:
  0.0 1066.6 jit_solution(15806059566089103764)
XLA Ops:
  12.4 4.5 collective-permute-start.1
  31.2 48.6 %all-gather.13.cloned.1.call-done = bf16[768,3352]{1,0:T(8,128)(2,1)} async-done(((bf16[24,3352]{1,0:T(8,128)(2,1)}), bf16[768,3352]{1,0:T(8,128)(2,1)}) %all-gather.13.cloned.1.call-update) | async-done | bytes 5148688 | tf_op jit(solution)/shard_map/all_gather | solution.py:201
  79.8 4.3 fusion.21
  125.8 3.3 fusion.65
  133.7 3.2 fusion.111
  140.2 3.2 collective-permute-start
  153.0 5.7 all_gather.59
  158.7 17.6 %all_gather.55 = bf16[4,1,24]{2,1,0:T(2,128)(2,1)} all-gather(bf16[1,1,24]{2,1,0:T(2,128)(2,1)} %get-tuple-element.980), channel_id=1, replica_groups=mesh['dp'=8,'ctx'=4] {'ctx'}, dimensions={0}, use_global_device_ids=true | all-gather | bytes 240 | tf_op jit(solution)/shard_map/all_gather | solution.py:36
  177.1 6.2 fusion.66
  192.5 3.6 fusion.108
  196.3 7.3 while.61
  206.2 8.5 fusion.82
  220.5 7.4 while.60
  230.5 8.6 fusion.83
  248.7 105.5 %reduce-scatter.5.cloned.1.call-done = f32[48,768]{1,0:T(8,128)} async-done(((f32[1536,768]{1,0:T(8,128)}), f32[48,768]{1,0:T(8,128)}) %reduce-scatter.5.cloned.1.call-update) | async-done | bytes 147472 | tf_op jit(solution)/shard_map/reduce_scatter | solution.py:317
  356.4 57.2 %all-gather.19.cloned.1.call-done = bf16[1536,768]{1,0:T(8,128)(2,1)} async-done(((bf16[48,768]{1,0:T(8,128)(2,1)}), bf16[1536,768]{1,0:T(8,128)(2,1)}) %all-gather.19.cloned.1.call-update) | async-done | bytes 2359312 | tf_op jit(solution)/shard_map/all_gather | solution.py:326
  413.6 3.5 fusion.22
  417.8 4.5 convolution_convert_fusion.11
  422.2 7.0 fusion.24
  429.2 4.4 convolution_convert_fusion.10
  433.6 6.8 add_convert_fusion.6
  440.5 4.6 convolution_convert_fusion.9
  445.1 6.9 add_convert_fusion.5
  452.0 4.4 convolution_convert_fusion.8
  456.4 6.9 add_convert_fusion.4
  463.3 4.4 convolution_convert_fusion.7
  467.7 6.9 fusion.171
  485.3 47.0 %all-gather.15.cloned.1.call-done = bf16[1536,768]{1,0:T(8,128)(2,1)} async-done(((bf16[48,768]{1,0:T(8,128)(2,1)}), bf16[1536,768]{1,0:T(8,128)(2,1)}) %all-gather.15.cloned.1.call-update) | async-done | bytes 2359312 | tf_op jit(solution)/shard_map/all_gather | solution.py:202
  532.3 4.0 fusion.84
  538.3 4.7 multiply_reduce_fusion.12
  548.7 3.6 convolution_convert_fusion.13
  552.3 6.3 multiply_reduce_fusion.13
  561.7 12.9 %fusion.28 = (f32[24,256]{1,0:T(8,128)}, f32[24,256]{1,0:T(8,128)}, f32[24,256]{1,0:T(8,128)}, f32[256,256]{1,0:T(8,128)S(1)}) fusion(f32[24,256]{1,0:T(8,128)S(1)} %copy-done.133, f32[256,256]{1,0:T(8,128)} %fusion.221, f32[256,256]{1,0:T(8,128)} %get-tuple-element.1007, f32[24,256]{1,0:T(8,128)S(1)} %copy-done.138, pred[256,256]{1,0:T(8,128)(4,1)S(1)} %copy-done.108, ...), kind=kOutput, calls=%fused_computation.56 | convolution fusion | flops 1231468544 | bytes 4120576 | tf_op jit(solution)/shard_map/transpose(jvp(bhts,bshp->bthp))/dot_general | solution.py:143
  577.7 3.3 mul.1547
  586.3 4.0 convolution_bitcast_fusion.3
  597.2 12.7 %fusion.26 = (f32[24,256]{1,0:T(8,128)}, f32[24,256]{1,0:T(8,128)}, f32[24,256]{1,0:T(8,128)}, f32[256,256]{1,0:T(8,128)S(1)}) fusion(f32[24,256]{1,0:T(8,128)} %copy.447, f32[256,256]{1,0:T(8,128)} %copy-done.84, f32[256,256]{1,0:T(8,128)} %get-tuple-element.1005, f32[24,256]{1,0:T(8,128)} %bitcast_add_fusion.14, ...), kind=kOutput, calls=%fused_computation.54 | convolution fusion | flops 1231468544 | bytes 4120576 | tf_op jit(solution)/shard_map/transpose(jvp(bhts,bshp->bthp))/dot_general | solution.py:143
  624.1 4.0 convolution_bitcast_fusion.5
  630.0 7.6 while.62
  639.0 3.5 fusion.90
  642.6 7.3 while.63
  653.1 6.8 fusion.80
  663.1 4.2 fusion.127
  667.3 8.4 fusion.81
  678.9 4.2 fusion.121
  683.2 4.4 multiply_reduce_fusion.11
  707.9 4.9 slice_add_fusion.1
  724.3 5.7 convolution_add_fusion
  730.2 143.8 %reduce-scatter.7.cloned.1.call-done = f32[24,3352]{1,0:T(8,128)} async-done(((f32[768,3352]{1,0:T(8,128)}), f32[24,3352]{1,0:T(8,128)}) %reduce-scatter.7.cloned.1.call-update) | async-done | bytes 321808
  883.9 4.4 fusion.170
  888.4 4.6 fusion.135
  893.0 42.5 %all-reduce.25 = (f32[768]{0:T(1024)S(1)}, f32[4,1792]{1,0:T(4,128)S(1)}, f32[1792]{0:T(1024)S(1)}, f32[24]{0:T(128)S(1)}, f32[24]{0:T(128)S(1)}, /*index=5*/f32[24]{0:T(128)S(1)}, f32[1536]{0:T(1024)S(1)}) all-reduce(f32[768]{0:T(1024)S(1)} %add.483, ...), channel_id=1, replica_groups=mesh['dp'=8,'ctx'=4] {'dp','ctx'}, use_global_device_ids=true, to_apply=%region_42.44 | all-reduce | flops 11336 | bytes 90688 | tf_op jit(solution)/shard_map/psum | solution.py:319
  942.3 8.0 copy.500
  950.3 5.7 fusion.4
  956.7 8.6 convolution_convert_fusion.6
  965.3 12.1 %add_convert_fusion.3 = bf16[768,3352]{0,1:T(8,128)(2,1)} fusion(bf16[768,768]{1,0:T(8,128)(2,1)S(1)} %convolution_convert_fusion.6, f32[]{:T(128)S(6)} %add.491, bf16[768,3352]{0,1:T(8,128)(2,1)} %copy.500), kind=kOutput, calls=%fused_computation.19 | convolution fusion | flops 4888842240 | bytes 11476996 | tf_op jit(solution)/shard_map/dot_general | solution.py:171
  977.4 8.2 convolution_convert_fusion.5
  985.6 10.6 add_convert_fusion.2
  996.1 7.9 convolution_convert_fusion.4
  1004.1 10.7 %add_convert_fusion.1 = bf16[768,3352]{0,1:T(8,128)(2,1)} fusion(bf16[768,3352]{0,1:T(8,128)(2,1)} %add_convert_fusion.2, bf16[768,768]{1,0:T(8,128)(2,1)S(1)} %convolution_convert_fusion.4), kind=kOutput, calls=%fused_computation.17 | convolution fusion | flops 4873396224 | bytes 11476992 | tf_op jit(solution)/shard_map/dot_general | solution.py:171
  1014.8 7.9 convolution_convert_fusion.3
  1022.7 10.6 add_convert_fusion
  1033.2 7.9 convolution_convert_fusion.2
  1041.2 10.9 %fusion.314 = f32[768,3352]{0,1:T(8,128)} fusion(bf16[768,3352]{0,1:T(8,128)(2,1)} %add_convert_fusion, bf16[768,768]{1,0:T(8,128)(2,1)S(1)} %convolution_convert_fusion.2), kind=kOutput, calls=%fused_computation.526 | convolution fusion | flops 4863098880 | bytes 16625664 | tf_op jit(solution)/shard_map/dot_general | solution.py:171
  1052.1 4.5 multiply_subtract_fusion
  (626 shorter events, 253.5 us)
Async XLA Ops:
  7.2 18.4 %copy-start.170 = (s32[2,256]{1,0:T(2,128)S(1)}, s32[2,256]{1,0:T(2,128)}, u32[]{:S(2)}) copy-start(s32[2,256]{1,0:T(2,128)} %param.24) | copy-start | bytes 6148
  7.2 72.6 %copy-start.31 = (bf16[2,256,768]{2,1,0:T(8,128)(2,1)S(1)}, bf16[2,256,768]{2,1,0:T(8,128)(2,1)}, u32[]{:S(2)}) copy-start(bf16[2,256,768]{2,1,0:T(8,128)(2,1)} %param.23) | copy-start | bytes 2359300
  7.2 72.6 %copy-start.61 = (f32[768]{0:T(1024)S(1)}, f32[768]{0:T(1024)}, u32[]{:S(2)}) copy-start(f32[768]{0:T(1024)} %param.30) | copy-start | bytes 9220
  7.2 72.5 %all-gather.13.cloned.1.call-start = ((), (), s32[]{:S(2)}) async-start(), calls=%async_computation.2 | async-start | bytes 5474304 | tf_op jit(solution)/shard_map/all_gather | solution.py:201
  9.0 187.2 %all-gather.23.cloned.1.call-start = ((), (), s32[]{:S(2)}) async-start(), calls=%async_computation.8 | async-start | bytes 1966080 | tf_op jit(solution)/shard_map/all_gather | solution.py:36
  9.9 14.5 %collective-permute-start.3 = (f32[1,3]{1,0:T(1,128)S(1)}, f32[1,3]{1,0:T(1,128)S(1)}, u32[]{:S(2)}, u32[]{:S(2)}) collective-permute-start(f32[1,3]{1,0:T(1,128)S(1)} %slice.264), channel_id=1, source_target_pairs={{0,1},{1,2},{2,3},{4,5},{5,6},{6,7},{8,9},{9,10},{10,11},{12,13},{... | collective-permute-start | bytes 44 | tf_op jit(solution)/shard_map/ppermute | solution.py:30
  12.4 12.6 %collective-permute-start.1 = (f32[1,3]{1,0:T(1,128)S(1)}, f32[1,3]{1,0:T(1,128)S(1)}, u32[]{:S(2)}, u32[]{:S(2)}) collective-permute-start(f32[1,3]{1,0:T(1,128)S(1)} %slice.244), channel_id=1, source_target_pairs={{0,1},{1,2},{2,3},{4,5},{5,6},{6,7},{8,9},{9,10},{10,11},{12,13},{... | collective-permute-start | bytes 44 | tf_op jit(solution)/shard_map/ppermute | solution.py:30
  20.8 156.3 %copy-start.98 = (f32[1792]{0:T(1024)}, f32[1792]{0:T(1024)S(1)}, u32[]{:S(2)}) copy-start(f32[1792]{0:T(1024)S(1)} %get-tuple-element.880) | copy-start | bytes 21508
  22.7 61.3 %copy-start.110 = (f32[256]{0:T(256)}, f32[256]{0:T(256)S(1)}, u32[]{:S(2)}) copy-start(f32[256]{0:T(256)S(1)} %fusion.262) | copy-start | bytes 3076
  22.8 61.5 %copy-start.150 = (f32[256]{0:T(256)}, f32[256]{0:T(256)S(1)}, u32[]{:S(2)}) copy-start(f32[256]{0:T(256)S(1)} %fusion.260) | copy-start | bytes 3076
  28.7 55.4 %copy-start.158 = (f32[1,256]{1,0:T(1,128)}, f32[1,256]{1,0:T(1,128)S(1)}, u32[]{:S(2)}) copy-start(f32[1,256]{1,0:T(1,128)S(1)} %get-tuple-element.992) | copy-start | bytes 3076
  28.7 55.4 %copy-start.160 = (f32[1,256]{1,0:T(1,128)}, f32[1,256]{1,0:T(1,128)S(1)}, u32[]{:S(2)}) copy-start(f32[1,256]{1,0:T(1,128)S(1)} %get-tuple-element.993) | copy-start | bytes 3076
  85.8 40.0 %copy-start.12 = (f32[1,256,1792]{2,1,0:T(8,128)}, f32[1,256,1792]{2,1,0:T(8,128)S(1)}, u32[]{:S(2)}) copy-start(f32[1,256,1792]{2,1,0:T(8,128)S(1)} %slice_convert_fusion.2) | copy-start | bytes 5505028
  103.1 21.9 %collective-permute-start.2 = (f32[1,3,1792]{2,0,1:T(1,128)}, f32[1,3,1792]{2,0,1:T(1,128)}, u32[]{:S(2)}, u32[]{:S(2)}) collective-permute-start(f32[1,3,1792]{2,0,1:T(1,128)} %copy.455), channel_id=1, source_target_pairs={{0,1},{1,2},{2,3},{4,5},{5,6},{6,7},{8,9},{9,10},{10,11},{12,13},{... | collective-permute-start | bytes 64520 | tf_op jit(solution)/shard_map/ppermute | solution.py:30
  112.1 5.8 copy-start.54
  113.2 7.4 copy-start.154
  133.7 72.4 %copy-start.3 = (f32[1,256,1536]{1,2,0:T(8,128)}, f32[1,256,1536]{1,2,0:T(8,128)S(1)}, u32[]{:S(2)}) copy-start(f32[1,256,1536]{1,2,0:T(8,128)S(1)} %copy.457) | copy-start | bytes 4718596
  136.9 11.5 %copy-start.65 = (f32[24,256]{0,1:T(8,128)S(1)}, f32[24,256]{0,1:T(8,128)}, u32[]{:S(2)}) copy-start(f32[24,256]{0,1:T(8,128)} %get-tuple-element.973) | copy-start | bytes 73732
  136.9 16.0 %copy-start.66 = (f32[256,24]{1,0:T(8,128)S(1)}, f32[256,24]{1,0:T(8,128)}, u32[]{:S(2)}) copy-start(f32[256,24]{1,0:T(8,128)} %get-tuple-element.951) | copy-start | bytes 73732
  136.9 83.5 %all-gather.21.cloned.1.call-start = ((), (), s32[]{:S(2)}) async-start(), calls=%async_computation.7 | async-start | bytes 1966080 | tf_op jit(solution)/shard_map/all_gather | solution.py:36
  137.0 6.5 copy-start.157
  140.2 36.2 %collective-permute-start = (f32[1,3,1792]{2,0,1:T(1,128)}, f32[1,3,1792]{2,0,1:T(1,128)}, u32[]{:S(2)}, u32[]{:S(2)}) collective-permute-start(f32[1,3,1792]{2,0,1:T(1,128)} %copy.441), channel_id=1, source_target_pairs={{0,1},{1,2},{2,3},{4,5},{5,6},{6,7},{8,9},{9,10},{10,11},{12,13},{... | collective-permute-start | bytes 64520 | tf_op jit(solution)/shard_map/ppermute | solution.py:30
  177.1 6.3 copy-start.90
  186.0 6.5 copy-start.94
  192.5 37.9 %copy-start.84 = (f32[256,256]{1,0:T(8,128)}, f32[256,256]{1,0:T(8,128)S(1)}, u32[]{:S(2)}) copy-start(f32[256,256]{1,0:T(8,128)S(1)} %fusion.230) | copy-start | bytes 786436
  196.2 158.1 %reduce-scatter.5.cloned.1.call-start = ((), (), s32[]{:S(2)}) async-start(), calls=%async_computation.4 | async-start | bytes 4866048 | tf_op jit(solution)/shard_map/reduce_scatter | solution.py:317
  206.1 8.6 copy-start.37
  219.8 24.5 %copy-start.6 = (f32[1,256,1536]{2,1,0:T(8,128)}, f32[1,256,1536]{2,1,0:T(8,128)S(1)}, u32[]{:S(2)}) copy-start(f32[1,256,1536]{2,1,0:T(8,128)S(1)} %get-tuple-element.956) | copy-start | bytes 4718596
  230.4 8.7 copy-start.43
  244.4 293.9 %copy-start.146 = (f32[256]{0:T(256)}, f32[256]{0:T(256)S(1)}, u32[]{:S(2)}) copy-start(f32[256]{0:T(256)S(1)} %fusion.261) | copy-start | bytes 3076
  248.7 105.6 %copy-start.96 = (f32[48,768]{1,0:T(8,128)S(1)}, f32[48,768]{1,0:T(8,128)}, u32[]{:S(2)}) copy-start(f32[48,768]{1,0:T(8,128)} %param.29) | copy-start | bytes 442372
  248.7 164.9 %all-gather.19.cloned.1.call-start = ((), (), s32[]{:S(2)}) async-start(), calls=%async_computation.6 | async-start | bytes 2433024 | tf_op jit(solution)/shard_map/all_gather | solution.py:326
  355.9 176.4 %all-gather.15.cloned.1.call-start = ((), (), s32[]{:S(2)}) async-start(), calls=%async_computation.3 | async-start | bytes 2433024 | tf_op jit(solution)/shard_map/all_gather | solution.py:202
  467.7 6.9 copy-start.97
  476.3 153.7 %all-gather.25.cloned.1.call-start = ((), (), s32[]{:S(2)}) async-start(), calls=%async_computation.9 | async-start | bytes 1966080 | tf_op jit(solution)/shard_map/all_gather | solution.py:59
  532.3 6.0 copy-start.10
  532.3 6.0 copy-start.19
  538.3 5.9 copy-start.46
  552.2 90.3 %all-gather.27.cloned.1.call-start = ((), (), s32[]{:S(2)}) async-start(), calls=%async_computation.10 | async-start | bytes 1966080 | tf_op jit(solution)/shard_map/all_gather | solution.py:59
  584.0 7.8 copy-start.39
  584.0 7.8 copy-start.44
  609.9 264.1 %reduce-scatter.7.cloned.1.call-start = ((), (), s32[]{:S(2)}) async-start(), calls=%async_computation.11 | async-start | bytes 10948608
  695.4 8.8 copy-start.72
  696.2 8.0 copy-start.70
  696.2 8.0 copy-start.71
  696.2 8.0 copy-start.159
  696.2 11.7 %copy-start.17 = (f32[1,256,1792]{2,1,0:T(8,128)S(1)}, f32[1,256,1792]{2,1,0:T(8,128)}, u32[]{:S(2)}) copy-start(f32[1,256,1792]{2,1,0:T(8,128)} %copy-done.16) | copy-start | bytes 5505028
  696.2 11.7 %copy-start.99 = (f32[1792]{0:T(1024)S(1)}, f32[1792]{0:T(1024)}, u32[]{:S(2)}) copy-start(f32[1792]{0:T(1024)} %copy-done.98) | copy-start | bytes 21508
  702.2 17.5 %collective-permute-start.4 = (f32[1,3,1792]{2,0,1:T(1,128)S(1)}, f32[1,3,1792]{2,0,1:T(1,128)S(1)}, u32[]{:S(2)}, u32[]{:S(2)}) collective-permute-start(f32[1,3,1792]{2,0,1:T(1,128)S(1)} %copy.475), channel_id=1, source_target_pairs={{1,0},{2,1},{3,2},{5,4},{6,5},{7,6},{9,8},{10,9},{11,10},{13,12},{... | collective-permute-start | bytes 64520 | tf_op jit(solution)/shard_map/ppermute | solution.py:30
  714.8 5.9 collective-permute-start.5
  730.1 144.0 %copy-start.76 = (f32[24,3352]{1,0:T(8,128)S(1)}, f32[24,3352]{1,0:T(8,128)}, u32[]{:S(2)}) copy-start(f32[24,3352]{1,0:T(8,128)} %param.28) | copy-start | bytes 965380
  730.1 145.8 %copy-start.60 = (f32[24,3352]{1,0:T(8,128)S(1)}, f32[24,3352]{1,0:T(8,128)}, u32[]{:S(2)}) copy-start(f32[24,3352]{1,0:T(8,128)} %param.26) | copy-start | bytes 965380
  730.1 147.6 %copy-start.124 = (f32[1536]{0:T(1024)S(1)}, f32[1536]{0:T(1024)}, u32[]{:S(2)}) copy-start(f32[1536]{0:T(1024)} %get-tuple-element.941) | copy-start | bytes 18436
  730.1 147.7 %copy-start.115 = (f32[1536]{0:T(1024)S(1)}, f32[1536]{0:T(1024)}, u32[]{:S(2)}) copy-start(f32[1536]{0:T(1024)} %get-tuple-element.939) | copy-start | bytes 18436
  730.1 147.9 %copy-start.112 = (f32[1536]{0:T(1024)S(1)}, f32[1536]{0:T(1024)}, u32[]{:S(2)}) copy-start(f32[1536]{0:T(1024)} %get-tuple-element.864) | copy-start | bytes 18436
  730.1 147.9 %copy-start.113 = (f32[1536]{0:T(1024)S(1)}, f32[1536]{0:T(1024)}, u32[]{:S(2)}) copy-start(f32[1536]{0:T(1024)} %get-tuple-element.989) | copy-start | bytes 18436
  730.1 147.9 %copy-start.8 = (f32[1,256,1536]{2,1,0:T(8,128)S(1)}, f32[1,256,1536]{2,1,0:T(8,128)}, u32[]{:S(2)}) copy-start(f32[1,256,1536]{2,1,0:T(8,128)} %copy-done.6) | copy-start | bytes 4718596
  730.1 147.9 %copy-start.149 = (f32[256]{0:T(256)S(1)}, f32[256]{0:T(256)}, u32[]{:S(2)}) copy-start(f32[256]{0:T(256)} %fusion.263) | copy-start | bytes 3076
  730.1 212.2 %all-gather.17.cloned.1.call-start = ((), (), s32[]{:S(2)}) async-start(), calls=%async_computation.5 | async-start | bytes 5474304 | tf_op jit(solution)/shard_map/all_gather | solution.py:325
  888.3 47.2 %copy-start.165 = (f32[256]{0:T(256)S(1)}, f32[256]{0:T(256)}, u32[]{:S(2)}) copy-start(f32[256]{0:T(256)} %copy-done.164) | copy-start | bytes 3076
  888.4 47.2 %copy-start.167 = (f32[256]{0:T(256)S(1)}, f32[256]{0:T(256)}, u32[]{:S(2)}) copy-start(f32[256]{0:T(256)} %copy-done.166) | copy-start | bytes 3076
  888.4 47.2 %copy-start.30 = (bf16[2,256,768]{2,1,0:T(8,128)(2,1)S(1)}, bf16[2,256,768]{2,1,0:T(8,128)(2,1)}, u32[]{:S(2)}) copy-start(bf16[2,256,768]{2,1,0:T(8,128)(2,1)} %param.25) | copy-start | bytes 2359300
  888.4 47.2 %copy-start.35 = (bf16[2,256,768]{2,1,0:T(8,128)(2,1)S(1)}, bf16[2,256,768]{2,1,0:T(8,128)(2,1)}, u32[]{:S(2)}) copy-start(bf16[2,256,768]{2,1,0:T(8,128)(2,1)} %param.23) | copy-start | bytes 2359300
  1041.2 10.9 %copy-start.36 = (f32[24,3352]{0,1:T(8,128)S(1)}, f32[24,3352]{0,1:T(8,128)}, u32[]{:S(2)}) copy-start(f32[24,3352]{0,1:T(8,128)} %copy.502) | copy-start | bytes 965380
  (139 other events, 391.6 us)
Sparse Core Ops, SparseCore 0:
  11.4 68.2 all-gather.12
  137.0 18.0 all-gather.22
  196.3 17.5 all-gather.20
  248.8 105.4 reduce-scatter.4
  357.6 55.9 all-gather.18
  476.5 55.8 all-gather.14
  552.4 18.4 all-gather.24
  610.0 18.4 all-gather.26
  730.2 143.7 reduce-scatter.6
  877.3 64.9 all-gather.16
where the time goes:
time: 1080 us; the launch traced here: 1070 us
  waiting for transfers between devices  404 us (37%)
  matrix products  298 us (28%)
  other arithmetic  146 us (14%)
  local copies, waits for them, and re-layouts  116 us (11%)
  blocking collectives  65.8 us (6%)
  between operations  18.7 us (2%)
  starting transfers between devices  16.7 us (2%)
    unnamed x11, waiting for transfers between devices  144 us
    reduce_scatter x1, waiting for transfers between devices, body(): lax.psum_scatter(acc_out, ('dp', 'ctx'), scatter_dimension=0, tiled=True)  106 us
    dot_general x10, matrix products, orthogonal(): jnp.dot(poly_mat, current, preferred_element_type=jnp.float32)  89.3 us
    dot_general x10, matrix products, orthogonal(): jnp.dot(current, current.T, preferred_element_type=jnp.float32)  62.8 us
    dot_general x6, matrix products, block_out(): jnp.einsum('bhts,bshp->bthp', weight, x_heads, precision=lax.Precision.HI...  57.9 us
    all_gather x1, waiting for transfers between devices, body(): lax.all_gather(next_mom_out.astype(jnp.bfloat16), ('dp', 'ctx'), axis=0,...  57.2 us
    all_gather x1, waiting for transfers between devices, body(): lax.all_gather(win_low, ('dp', 'ctx'), axis=0, tiled=True)  48.6 us
    all_gather x1, waiting for transfers between devices, body(): lax.all_gather(wout_low, ('dp', 'ctx'), axis=0, tiled=True)  47 us
  transfers between devices with their start and end apart: 16, of which 6 were waited for; matrix products, arithmetic and copies ran while one was open for 21% of the time, Pallas kernels for 0%

commit v1 on v0

--- a/solution.py
+++ b/solution.py
@@ -199,7 +199,12 @@
         micro_rows = slice(micro_idx * SEQ_MB, (micro_idx + 1) * SEQ_MB)
         full_in, full_out = (
             lax.all_gather(win_low, ("dp", "ctx"), axis=0, tiled=True),
-            lax.all_gather(wout_low, ("dp", "ctx"), axis=0, tiled=True),
+            jnp.concatenate(
+                lax.all_to_all(
+                    jnp.stack([wout_low] * lax.axis_size(("dp", "ctx"))), ("dp", "ctx"), 0, 0
+                ),
+                axis=0,
+            ),
         )
         x_float = tokens[micro_rows].astype(jnp.float32)
         seg_float = segment_ids[micro_rows].astype(jnp.float32)

time: 1080 us -> 1160 us (1.074)
  waiting for transfers between devices: 404 us -> 479 us
    all_to_all x0 -> x1, waiting for transfers between devices: none -> 77 us  [body(): lax.all_to_all(jnp.stack([wout_low] * lax.axis_size(('dp', 'ctx'))), ('dp...]
  transfers between devices with their start and end apart: 16 -> 17, of which waited for: 6 -> 6; matrix products, arithmetic and copies ran while one was open for 21% -> 20% of each run, Pallas kernels for 0% -> 0%
where the time goes in v1:
time: 1160 us; the launch traced here: 1140 us
  waiting for transfers between devices  479 us (41%)
  matrix products  300 us (26%)
  other arithmetic  146 us (13%)
  local copies, waits for them, and re-layouts  117 us (10%)
  blocking collectives  62.8 us (5%)
  starting transfers between devices  20.4 us (2%)
  between operations  18.4 us (2%)
    unnamed x11, waiting for transfers between devices  144 us
    reduce_scatter x1, waiting for transfers between devices, body(): lax.psum_scatter(acc_out, ('dp', 'ctx'), scatter_dimension=0, tiled=True)  106 us
    dot_general x10, matrix products, orthogonal(): jnp.dot(poly_mat, current, preferred_element_type=jnp.float32)  89.2 us
    all_to_all x1, waiting for transfers between devices, body(): lax.all_to_all(jnp.stack([wout_low] * lax.axis_size(('dp', 'ctx'))), ('dp...  77 us
    dot_general x10, matrix products, orthogonal(): jnp.dot(current, current.T, preferred_element_type=jnp.float32)  63 us
    dot_general x6, matrix products, block_out(): jnp.einsum('bhts,bshp->bthp', weight, x_heads, precision=lax.Precision.HI...  57.9 us
    all_gather x1, waiting for transfers between devices, body(): lax.all_gather(next_mom_out.astype(jnp.bfloat16), ('dp', 'ctx'), axis=0,...  57.2 us
    all_gather x1, waiting for transfers between devices, body(): lax.all_gather(win_low, ('dp', 'ctx'), axis=0, tiled=True)  48.4 us
  transfers between devices with their start and end apart: 17, of which 6 were waited for; matrix products, arithmetic and copies ran while one was open for 20% of the time, Pallas kernels for 0%

profile of v1, /device:TPU:0, one launch (start us, length us, event | category | flops | bytes accessed | tf_op | source)
XLA Modules:
  0.0 1144.4 jit_solution(1560762918955842990)
XLA Ops:
  12.4 4.5 collective-permute-start.1
  31.4 48.4 %all-gather.13.cloned.1.call-done = bf16[768,3352]{1,0:T(8,128)(2,1)} async-done(((bf16[24,3352]{1,0:T(8,128)(2,1)}), bf16[768,3352]{1,0:T(8,128)(2,1)}) %all-gather.13.cloned.1.call-update) | async-done | bytes 5148688 | tf_op jit(solution)/shard_map/all_gather | solution.py:201
  79.8 4.3 fusion.21
  125.9 3.3 fusion.65
  140.2 3.2 collective-permute-start
  153.1 5.1 all_gather.56
  158.2 18.8 %all_gather.53 = bf16[4,1,24]{2,1,0:T(2,128)(2,1)} all-gather(bf16[1,1,24]{2,1,0:T(2,128)(2,1)} %get-tuple-element.980), channel_id=1, replica_groups=mesh['dp'=8,'ctx'=4] {'ctx'}, dimensions={0}, use_global_device_ids=true | all-gather | bytes 240 | tf_op jit(solution)/shard_map/all_gather | solution.py:36
  177.7 6.2 fusion.66
  193.1 3.6 fusion.108
  196.9 7.3 while.61
  206.8 8.5 fusion.82
  221.1 7.2 while.60
  231.0 8.6 fusion.83
  249.2 105.5 %reduce-scatter.5.cloned.1.call-done = f32[48,768]{1,0:T(8,128)} async-done(((f32[1536,768]{1,0:T(8,128)}), f32[48,768]{1,0:T(8,128)}) %reduce-scatter.5.cloned.1.call-update) | async-done | bytes 147472 | tf_op jit(solution)/shard_map/reduce_scatter | solution.py:322
  356.8 57.2 %all-gather.19.cloned.1.call-done = bf16[1536,768]{1,0:T(8,128)(2,1)} async-done(((bf16[48,768]{1,0:T(8,128)(2,1)}), bf16[1536,768]{1,0:T(8,128)(2,1)}) %all-gather.19.cloned.1.call-update) | async-done | bytes 2359312 | tf_op jit(solution)/shard_map/all_gather | solution.py:331
  414.0 3.5 fusion.22
  418.2 4.5 convolution_convert_fusion.11
  422.6 7.0 fusion.24
  429.7 4.4 convolution_convert_fusion.10
  434.1 6.8 add_convert_fusion.6
  440.9 4.6 convolution_convert_fusion.9
  445.5 6.9 add_convert_fusion.5
  452.5 4.4 convolution_convert_fusion.8
  456.9 6.9 add_convert_fusion.4
  463.8 4.4 convolution_convert_fusion.7
  468.3 6.9 fusion.171
  485.8 47.1 %all-gather.15.cloned.1.call-done = bf16[1536,768]{1,0:T(8,128)(2,1)} async-done(((bf16[48,768]{1,0:T(8,128)(2,1)}), bf16[1536,768]{1,0:T(8,128)(2,1)}) %all-gather.15.cloned.1.call-update) | async-done | bytes 2359312 | tf_op jit(solution)/shard_map/all_gather | solution.py:273
  532.9 4.0 fusion.84
  538.9 4.7 multiply_reduce_fusion.12
  549.1 3.6 convolution_convert_fusion.13
  552.8 6.3 multiply_reduce_fusion.13
  562.2 12.9 %fusion.28 = (f32[24,256]{1,0:T(8,128)}, f32[24,256]{1,0:T(8,128)}, f32[24,256]{1,0:T(8,128)}, f32[256,256]{1,0:T(8,128)S(1)}) fusion(f32[24,256]{1,0:T(8,128)S(1)} %copy-done.133, f32[256,256]{1,0:T(8,128)} %fusion.221, f32[256,256]{1,0:T(8,128)} %get-tuple-element.1007, f32[24,256]{1,0:T(8,128)S(1)} %copy-done.138, pred[256,256]{1,0:T(8,128)(4,1)S(1)} %copy-done.108, ...), kind=kOutput, calls=%fused_computation.56 | convolution fusion | flops 1231468544 | bytes 4120576 | tf_op jit(solution)/shard_map/transpose(jvp(bhts,bshp->bthp))/dot_general | solution.py:143
  586.7 4.0 convolution_bitcast_fusion.3
  597.6 12.7 %fusion.26 = (f32[24,256]{1,0:T(8,128)}, f32[24,256]{1,0:T(8,128)}, f32[24,256]{1,0:T(8,128)}, f32[256,256]{1,0:T(8,128)S(1)}) fusion(f32[24,256]{1,0:T(8,128)} %copy.447, f32[256,256]{1,0:T(8,128)} %copy-done.84, f32[256,256]{1,0:T(8,128)} %get-tuple-element.1005, f32[24,256]{1,0:T(8,128)} %bitcast_add_fusion.14, ...), kind=kOutput, calls=%fused_computation.54 | convolution fusion | flops 1231468544 | bytes 4120576 | tf_op jit(solution)/shard_map/transpose(jvp(bhts,bshp->bthp))/dot_general | solution.py:143
  624.4 4.0 convolution_bitcast_fusion.5
  630.4 7.5 while.62
  639.3 3.4 fusion.90
  642.7 7.3 while.63
  653.3 6.8 fusion.80
  663.2 4.2 fusion.127
  667.5 8.4 fusion.81
  678.9 4.2 fusion.121
  683.3 4.4 multiply_reduce_fusion.11
  708.0 4.9 slice_add_fusion.1
  724.4 5.7 convolution_add_fusion
  730.2 143.9 %reduce-scatter.7.cloned.1.call-done = f32[24,3352]{1,0:T(8,128)} async-done(((f32[768,3352]{1,0:T(8,128)}), f32[24,3352]{1,0:T(8,128)}) %reduce-scatter.7.cloned.1.call-update) | async-done | bytes 321808
  877.5 3.7 all-to-all-start
  883.5 77.0 %all-to-all-done = bf16[32,48,768]{2,1,0:T(8,128)(2,1)} async-done(((bf16[32,48,768]{2,1,0:T(8,128)(2,1)}), bf16[32,48,768]{2,1,0:T(8,128)(2,1)}, u32[]{:S(2)}, u32[]{:S(2)}) %all-to-all-start) | async-done | bytes 2359328 | tf_op jit(solution)/shard_map/all_to_all | solution.py:203
  967.6 4.3 fusion.170
  972.0 4.6 fusion.135
  976.6 38.9 %all-reduce.25 = (f32[768]{0:T(1024)S(1)}, f32[4,1792]{1,0:T(4,128)S(1)}, f32[1792]{0:T(1024)S(1)}, f32[24]{0:T(128)S(1)}, f32[24]{0:T(128)S(1)}, /*index=5*/f32[24]{0:T(128)S(1)}, f32[1536]{0:T(1024)S(1)}) all-reduce(f32[768]{0:T(1024)S(1)} %add.483, ...), channel_id=1, replica_groups=mesh['dp'=8,'ctx'=4] {'dp','ctx'}, use_global_device_ids=true, to_apply=%region_42.44 | all-reduce | flops 11336 | bytes 90688 | tf_op jit(solution)/shard_map/psum | solution.py:324
  1020.6 8.0 copy.500
  1028.6 5.7 fusion.4
  1035.0 8.6 convolution_convert_fusion.6
  1043.5 12.2 %add_convert_fusion.3 = bf16[768,3352]{0,1:T(8,128)(2,1)} fusion(bf16[768,768]{1,0:T(8,128)(2,1)S(1)} %convolution_convert_fusion.6, f32[]{:T(128)S(6)} %add.491, bf16[768,3352]{0,1:T(8,128)(2,1)} %copy.500), kind=kOutput, calls=%fused_computation.19 | convolution fusion | flops 4888842240 | bytes 11476996 | tf_op jit(solution)/shard_map/dot_general | solution.py:171
  1055.7 8.3 convolution_convert_fusion.5
  1064.0 10.5 add_convert_fusion.2
  1074.6 7.9 convolution_convert_fusion.4
  1082.5 10.6 add_convert_fusion.1
  1093.1 7.9 convolution_convert_fusion.3
  1101.1 10.5 add_convert_fusion
  1111.6 7.9 convolution_convert_fusion.2
  1119.5 10.7 fusion.314
  1130.3 4.5 multiply_subtract_fusion
  (629 shorter events, 260.9 us)
Async XLA Ops:
  7.2 18.5 %copy-start.170 = (s32[2,256]{1,0:T(2,128)S(1)}, s32[2,256]{1,0:T(2,128)}, u32[]{:S(2)}) copy-start(s32[2,256]{1,0:T(2,128)} %param.24) | copy-start | bytes 6148
  7.2 72.6 %copy-start.30 = (bf16[2,256,768]{2,1,0:T(8,128)(2,1)S(1)}, bf16[2,256,768]{2,1,0:T(8,128)(2,1)}, u32[]{:S(2)}) copy-start(bf16[2,256,768]{2,1,0:T(8,128)(2,1)} %param.23) | copy-start | bytes 2359300
  7.2 72.6 %copy-start.61 = (f32[768]{0:T(1024)S(1)}, f32[768]{0:T(1024)}, u32[]{:S(2)}) copy-start(f32[768]{0:T(1024)} %param.30) | copy-start | bytes 9220
  7.2 72.5 %all-gather.13.cloned.1.call-start = ((), (), s32[]{:S(2)}) async-start(), calls=%async_computation.3 | async-start | bytes 5474304 | tf_op jit(solution)/shard_map/all_gather | solution.py:201
  9.0 187.8 %all-gather.23.cloned.1.call-start = ((), (), s32[]{:S(2)}) async-start(), calls=%async_computation.9 | async-start | bytes 1966080 | tf_op jit(solution)/shard_map/all_gather | solution.py:36
  9.9 14.6 %collective-permute-start.3 = (f32[1,3]{1,0:T(1,128)S(1)}, f32[1,3]{1,0:T(1,128)S(1)}, u32[]{:S(2)}, u32[]{:S(2)}) collective-permute-start(f32[1,3]{1,0:T(1,128)S(1)} %slice.264), channel_id=1, source_target_pairs={{0,1},{1,2},{2,3},{4,5},{5,6},{6,7},{8,9},{9,10},{10,11},{12,13},{... | collective-permute-start | bytes 44 | tf_op jit(solution)/shard_map/ppermute | solution.py:30
  12.4 12.7 %collective-permute-start.1 = (f32[1,3]{1,0:T(1,128)S(1)}, f32[1,3]{1,0:T(1,128)S(1)}, u32[]{:S(2)}, u32[]{:S(2)}) collective-permute-start(f32[1,3]{1,0:T(1,128)S(1)} %slice.244), channel_id=1, source_target_pairs={{0,1},{1,2},{2,3},{4,5},{5,6},{6,7},{8,9},{9,10},{10,11},{12,13},{... | collective-permute-start | bytes 44 | tf_op jit(solution)/shard_map/ppermute | solution.py:30
  20.9 156.8 %copy-start.98 = (f32[1792]{0:T(1024)}, f32[1792]{0:T(1024)S(1)}, u32[]{:S(2)}) copy-start(f32[1792]{0:T(1024)S(1)} %get-tuple-element.880) | copy-start | bytes 21508
  22.8 61.2 %copy-start.110 = (f32[256]{0:T(256)}, f32[256]{0:T(256)S(1)}, u32[]{:S(2)}) copy-start(f32[256]{0:T(256)S(1)} %fusion.262) | copy-start | bytes 3076
  22.9 61.4 %copy-start.150 = (f32[256]{0:T(256)}, f32[256]{0:T(256)S(1)}, u32[]{:S(2)}) copy-start(f32[256]{0:T(256)S(1)} %fusion.260) | copy-start | bytes 3076
  28.9 55.2 %copy-start.158 = (f32[1,256]{1,0:T(1,128)}, f32[1,256]{1,0:T(1,128)S(1)}, u32[]{:S(2)}) copy-start(f32[1,256]{1,0:T(1,128)S(1)} %get-tuple-element.992) | copy-start | bytes 3076
  28.9 55.2 %copy-start.160 = (f32[1,256]{1,0:T(1,128)}, f32[1,256]{1,0:T(1,128)S(1)}, u32[]{:S(2)}) copy-start(f32[1,256]{1,0:T(1,128)S(1)} %get-tuple-element.993) | copy-start | bytes 3076
  85.8 40.0 %copy-start.12 = (f32[1,256,1792]{2,1,0:T(8,128)}, f32[1,256,1792]{2,1,0:T(8,128)S(1)}, u32[]{:S(2)}) copy-start(f32[1,256,1792]{2,1,0:T(8,128)S(1)} %slice_convert_fusion.2) | copy-start | bytes 5505028
  103.1 22.0 %collective-permute-start.2 = (f32[1,3,1792]{2,0,1:T(1,128)}, f32[1,3,1792]{2,0,1:T(1,128)}, u32[]{:S(2)}, u32[]{:S(2)}) collective-permute-start(f32[1,3,1792]{2,0,1:T(1,128)} %copy.455), channel_id=1, source_target_pairs={{0,1},{1,2},{2,3},{4,5},{5,6},{6,7},{8,9},{9,10},{10,11},{12,13},{... | collective-permute-start | bytes 64520 | tf_op jit(solution)/shard_map/ppermute | solution.py:30
  110.4 4.5 copy-start.156
  112.0 5.8 copy-start.53
  113.2 7.4 copy-start.154
  133.7 73.0 %copy-start.3 = (f32[1,256,1536]{1,2,0:T(8,128)}, f32[1,256,1536]{1,2,0:T(8,128)S(1)}, u32[]{:S(2)}) copy-start(f32[1,256,1536]{1,2,0:T(8,128)S(1)} %copy.457) | copy-start | bytes 4718596
  136.9 11.6 %copy-start.65 = (f32[24,256]{0,1:T(8,128)S(1)}, f32[24,256]{0,1:T(8,128)}, u32[]{:S(2)}) copy-start(f32[24,256]{0,1:T(8,128)} %get-tuple-element.973) | copy-start | bytes 73732
  137.0 16.1 %copy-start.66 = (f32[256,24]{1,0:T(8,128)S(1)}, f32[256,24]{1,0:T(8,128)}, u32[]{:S(2)}) copy-start(f32[256,24]{1,0:T(8,128)} %get-tuple-element.951) | copy-start | bytes 73732
  137.0 84.1 %all-gather.21.cloned.1.call-start = ((), (), s32[]{:S(2)}) async-start(), calls=%async_computation.8 | async-start | bytes 1966080 | tf_op jit(solution)/shard_map/all_gather | solution.py:36
  137.0 6.5 copy-start.157
  140.2 36.7 %collective-permute-start = (f32[1,3,1792]{2,0,1:T(1,128)}, f32[1,3,1792]{2,0,1:T(1,128)}, u32[]{:S(2)}, u32[]{:S(2)}) collective-permute-start(f32[1,3,1792]{2,0,1:T(1,128)} %copy.441), channel_id=1, source_target_pairs={{0,1},{1,2},{2,3},{4,5},{5,6},{6,7},{8,9},{9,10},{10,11},{12,13},{... | collective-permute-start | bytes 64520 | tf_op jit(solution)/shard_map/ppermute | solution.py:30
  177.7 6.3 copy-start.90
  186.6 6.5 copy-start.94
  193.1 37.8 %copy-start.84 = (f32[256,256]{1,0:T(8,128)}, f32[256,256]{1,0:T(8,128)S(1)}, u32[]{:S(2)}) copy-start(f32[256,256]{1,0:T(8,128)S(1)} %fusion.230) | copy-start | bytes 786436
  196.8 157.9 %reduce-scatter.5.cloned.1.call-start = ((), (), s32[]{:S(2)}) async-start(), calls=%async_computation.5 | async-start | bytes 4866048 | tf_op jit(solution)/shard_map/reduce_scatter | solution.py:322
  206.7 8.6 copy-start.36
  220.4 24.4 %copy-start.6 = (f32[1,256,1536]{2,1,0:T(8,128)}, f32[1,256,1536]{2,1,0:T(8,128)S(1)}, u32[]{:S(2)}) copy-start(f32[1,256,1536]{2,1,0:T(8,128)S(1)} %get-tuple-element.956) | copy-start | bytes 4718596
  230.9 8.6 copy-start.42
  244.8 294.0 %copy-start.146 = (f32[256]{0:T(256)}, f32[256]{0:T(256)S(1)}, u32[]{:S(2)}) copy-start(f32[256]{0:T(256)S(1)} %fusion.261) | copy-start | bytes 3076
  249.1 105.6 %copy-start.96 = (f32[48,768]{1,0:T(8,128)S(1)}, f32[48,768]{1,0:T(8,128)}, u32[]{:S(2)}) copy-start(f32[48,768]{1,0:T(8,128)} %param.29) | copy-start | bytes 442372
  249.1 164.9 %all-gather.19.cloned.1.call-start = ((), (), s32[]{:S(2)}) async-start(), calls=%async_computation.7 | async-start | bytes 2433024 | tf_op jit(solution)/shard_map/all_gather | solution.py:331
  356.4 176.5 %all-gather.15.cloned.1.call-start = ((), (), s32[]{:S(2)}) async-start(), calls=%async_computation.4 | async-start | bytes 2433024 | tf_op jit(solution)/shard_map/all_gather | solution.py:273
  468.3 6.9 copy-start.97
  476.9 153.5 %all-gather.25.cloned.1.call-start = ((), (), s32[]{:S(2)}) async-start(), calls=%async_computation.10 | async-start | bytes 1966080 | tf_op jit(solution)/shard_map/all_gather | solution.py:59
  532.9 6.0 copy-start.10
  532.9 6.0 copy-start.19
  538.8 4.8 copy-start.22
  538.9 5.9 copy-start.45
  552.7 90.0 %all-gather.27.cloned.1.call-start = ((), (), s32[]{:S(2)}) async-start(), calls=%async_computation.11 | async-start | bytes 1966080 | tf_op jit(solution)/shard_map/all_gather | solution.py:59
  584.4 7.8 copy-start.38
  584.4 7.8 copy-start.43
  610.3 263.7 %reduce-scatter.7.cloned.1.call-start = ((), (), s32[]{:S(2)}) async-start(), calls=%async_computation.12 | async-start | bytes 10948608
  695.5 8.8 copy-start.72
  696.3 8.0 copy-start.70
  696.3 8.0 copy-start.71
  696.3 8.0 copy-start.159
  696.3 11.7 %copy-start.17 = (f32[1,256,1792]{2,1,0:T(8,128)S(1)}, f32[1,256,1792]{2,1,0:T(8,128)}, u32[]{:S(2)}) copy-start(f32[1,256,1792]{2,1,0:T(8,128)} %copy-done.16) | copy-start | bytes 5505028
  696.3 11.7 %copy-start.99 = (f32[1792]{0:T(1024)S(1)}, f32[1792]{0:T(1024)}, u32[]{:S(2)}) copy-start(f32[1792]{0:T(1024)} %copy-done.98) | copy-start | bytes 21508
  702.3 17.5 %collective-permute-start.4 = (f32[1,3,1792]{2,0,1:T(1,128)S(1)}, f32[1,3,1792]{2,0,1:T(1,128)S(1)}, u32[]{:S(2)}, u32[]{:S(2)}) collective-permute-start(f32[1,3,1792]{2,0,1:T(1,128)S(1)} %copy.475), channel_id=1, source_target_pairs={{1,0},{2,1},{3,2},{5,4},{6,5},{7,6},{9,8},{10,9},{11,10},{13,12},{... | collective-permute-start | bytes 64520 | tf_op jit(solution)/shard_map/ppermute | solution.py:30
  713.2 4.9 copy-start.69
  714.9 5.9 collective-permute-start.5
  730.1 144.0 %copy-start.76 = (f32[24,3352]{1,0:T(8,128)S(1)}, f32[24,3352]{1,0:T(8,128)}, u32[]{:S(2)}) copy-start(f32[24,3352]{1,0:T(8,128)} %param.28) | copy-start | bytes 965380
  730.1 145.8 %copy-start.60 = (bf16[48,768]{1,0:T(8,128)(2,1)S(1)}, bf16[48,768]{1,0:T(8,128)(2,1)}, u32[]{:S(2)}) copy-start(bf16[48,768]{1,0:T(8,128)(2,1)} %get-tuple-element.978) | copy-start | bytes 221188
  730.1 290.5 %all-gather.17.cloned.1.call-start = ((), (), s32[]{:S(2)}) async-start(), calls=%async_computation.6 | async-start | bytes 5474304 | tf_op jit(solution)/shard_map/all_gather | solution.py:330
  877.5 83.0 %all-to-all-start = ((bf16[32,48,768]{2,1,0:T(8,128)(2,1)}), bf16[32,48,768]{2,1,0:T(8,128)(2,1)}, u32[]{:S(2)}, u32[]{:S(2)}) async-start(bf16[32,48,768]{2,1,0:T(8,128)(2,1)} %stack.2), calls=%async_computation | async-start | bytes 4718592 | tf_op jit(solution)/shard_map/all_to_all | solution.py:203
  881.3 79.2 %copy-start.8 = (f32[1,256,1536]{2,1,0:T(8,128)S(1)}, f32[1,256,1536]{2,1,0:T(8,128)}, u32[]{:S(2)}) copy-start(f32[1,256,1536]{2,1,0:T(8,128)} %copy-done.6) | copy-start | bytes 4718596
  881.3 79.2 %copy-start.149 = (f32[256]{0:T(256)S(1)}, f32[256]{0:T(256)}, u32[]{:S(2)}) copy-start(f32[256]{0:T(256)} %fusion.263) | copy-start | bytes 3076
  972.0 43.6 %copy-start.165 = (f32[256]{0:T(256)S(1)}, f32[256]{0:T(256)}, u32[]{:S(2)}) copy-start(f32[256]{0:T(256)} %copy-done.164) | copy-start | bytes 3076
  972.0 43.6 %copy-start.167 = (f32[256]{0:T(256)S(1)}, f32[256]{0:T(256)}, u32[]{:S(2)}) copy-start(f32[256]{0:T(256)} %copy-done.166) | copy-start | bytes 3076
  972.0 43.6 %copy-start.29 = (bf16[2,256,768]{2,1,0:T(8,128)(2,1)S(1)}, bf16[2,256,768]{2,1,0:T(8,128)(2,1)}, u32[]{:S(2)}) copy-start(bf16[2,256,768]{2,1,0:T(8,128)(2,1)} %param.25) | copy-start | bytes 2359300
  972.0 43.6 %copy-start.34 = (bf16[2,256,768]{2,1,0:T(8,128)(2,1)S(1)}, bf16[2,256,768]{2,1,0:T(8,128)(2,1)}, u32[]{:S(2)}) copy-start(bf16[2,256,768]{2,1,0:T(8,128)(2,1)} %param.23) | copy-start | bytes 2359300
  1119.5 10.7 copy-start.35
  (140 other events, 407.3 us)
Sparse Core Ops, SparseCore 0:
  11.4 68.2 all-gather.12
  137.1 18.0 all-gather.22
  196.9 17.5 all-gather.20
  249.2 105.4 reduce-scatter.4
  358.0 55.9 all-gather.18
  477.0 55.8 all-gather.14
  552.8 18.4 all-gather.24
  610.5 18.4 all-gather.26
  730.2 143.7 reduce-scatter.6
  877.3 83.9 all-gather.16
